TPU v7x, 32 devices: a whole 2x2x4 slice. The times are simulated.
32 devices in a mesh: grp: 2 (over x), scan: 8 (over z, y), det: 2 (over core).
Axes of the slice: x: 2, y: 2, z: 4, core: 2. Of those that a mesh axis runs over, the one named last changes fastest.
Arguments:
- spectra: float32 [16384, 4096], P(('grp', 'scan'), 'det'), parts along dimension 0, may hold values from 0 to 544, as said below
- basis: float32 [64, 4096], P('grp', 'det'), parts along dimension 0, may hold values from 0.03 to 8, as said below
- loadings: float32 [64, 8192], P('grp', 'scan'), parts along dimension 0, may hold values from 0.005 to 6, as said below
Outputs:
- new_loadings: float32 [64, 8192], P('grp', 'scan'), parts along dimension 0
- new_basis: float32 [64, 4096], P('grp', 'det'), parts along dimension 0
There are 2 independent parts, one for each index of `grp`. A program takes and returns all parts, laid end to end along the dimension named above; each array names one. Nothing has to cross between parts.
Inputs may be any that keep to these rules, and one draw needn't show every extreme that they name: `spectra`: intensities are nonnegative. `basis`: entries are positive. `loadings`: entries are positive.
All inputs are finite; a program needn't handle non-finite values.
Results may differ from a plain program's by a relative error of at most 0.00005.
Values sent between devices are 32-bit elements; how exact they have to be, the bound alone decides.
A program may use at most 64 MiB of HBM per device.

v0:
```python
import functools

import jax
import jax.numpy as jnp
from jax import lax
from jax.experimental import pallas as pl
from jax.experimental.pallas import tpu as pltpu
from jax.sharding import PartitionSpec as P

HIGHEST = lax.Precision.HIGHEST
MESH = pl.DeviceIdType.MESH
F32 = jnp.float32
BF16 = jnp.bfloat16
LANES = 128


def split(x):
    hi = x.astype(BF16)
    lo = (x - hi.astype(F32)).astype(BF16)
    return hi, lo


def dot_nt(a, b):
    return lax.dot_general(a, b, (((1,), (1,)), ((), ())), preferred_element_type=F32)


def dot_nn(a, b):
    return lax.dot_general(a, b, (((1,), (0,)), ((), ())), preferred_element_type=F32)


def mirrored(x):
    index = (LANES - 1) - lax.broadcasted_iota(jnp.int32, x.shape, 1)
    return jnp.take_along_axis(x, index, axis=1, mode="promise_in_bounds")


def remote(src, dst, send, recv, where):
    return pltpu.make_async_remote_copy(
        src_ref=src, dst_ref=dst, send_sem=send, recv_sem=recv,
        device_id=where, device_id_type=MESH,
    )


def layout(n, rank, pixels):
    half = pixels // LANES // 2
    if n <= half:
        per, row_split = half // n, 1
    else:
        per, row_split = 1, min(n // half, rank // 8)
    return half, per, row_split


def piece_at(index, per, row_split, rows):
    first = index // row_split * per
    row = pl.multiple_of(lax.rem(index, row_split) * rows, 8) if row_split > 1 else 0
    return pl.ds(first, per), pl.ds(row, rows)


def tie_kernel(
    load_chunks, early,
    spectra, basis, loadings,
    s_hi, s_lo, tied3, tied2, load, weighted,
    sbuf, own, other, sp_sem, io_sem, bs_sem,
):
    rank, pixels = basis.shape
    positions = loadings.shape[1]
    blocks = pixels // LANES
    partner = {"det": 1 - lax.axis_index("det")}
    barrier = pltpu.get_barrier_semaphore()
    pl.semaphore_signal(barrier, inc=1, device_id=partner, device_id_type=MESH)

    load_rows = positions // load_chunks
    spectra_copies = []
    for i in range(load_chunks):
        part = pl.ds(i * load_rows, load_rows)
        spectra_copies.append(
            pltpu.make_async_copy(spectra.at[part], sbuf.at[part], sp_sem.at[i])
        )
    own_copy = pltpu.make_async_copy(basis, own, io_sem.at[0])
    load_copy = pltpu.make_async_copy(loadings, load, io_sem.at[1])
    basis_copy = remote(basis, other, bs_sem.at[0], bs_sem.at[1], partner)
    for i in range(early):
        spectra_copies[i].start()
    pl.semaphore_wait(barrier, 1)
    basis_copy.start()
    own_copy.start()
    load_copy.start()
    for i in range(early, load_chunks):
        spectra_copies[i].start()

    def divide(i):
        spectra_copies[i].wait()

        @pl.loop(0, load_rows // 16, unroll=True)
        def _(j):
            part = pl.ds(pl.multiple_of(i * load_rows + j * 16, 16), 16)
            hi, lo = split(sbuf[part, :])
            s_hi[part, :] = hi
            s_lo[part, :] = lo

    for i in range(early):
        divide(i)
    own_copy.wait()
    basis_copy.wait()
    for b in range(blocks):
        mine = own[:, b * LANES:(b + 1) * LANES]
        back = blocks - 1 - b
        tied = 0.5 * (mine + mirrored(other[:, back * LANES:(back + 1) * LANES]))
        tied3[b] = tied
        hi, lo = split(tied)
        tied2[:rank, b * LANES:(b + 1) * LANES] = hi
        tied2[rank:, b * LANES:(b + 1) * LANES] = lo
    squares = dot_nt(tied2[...], tied2[...])
    gram = 2.0 * (
        squares[:rank, :rank] + (squares[:rank, rank:] + squares[rank:, :rank])
    )
    load_copy.wait()
    weighted[...] = jnp.dot(
        gram, load[...], precision=HIGHEST, preferred_element_type=F32
    )
    for i in range(early, load_chunks):
        divide(i)


def update_kernel(
    n, pos_chunk, col_chunk, wait_at,
    s_hi, s_lo, tied3, tied2, load, weighted,
    new_loadings, piece_buf, ag_in, fw_in,
    nl2, num_out, num_in, w_keep, w_out, w_in, rs_in, cr_out, cr_in,
    nm_sem, w_sem, rs_send, rs_recv, cr_send, cr_recv,
    ag_send, ag_recv, fw_send, fw_recv,
):
    blocks, rank, _ = tied3.shape
    half, per, row_split = layout(n, rank, blocks * LANES)
    owners = half // per * row_split
    rows = rank // row_split
    pack = LANES // rank
    me = lax.axis_index("scan")
    partner = {"det": 1 - lax.axis_index("det")}

    def peer(k):
        return lax.rem(me + k, n)

    def source(k):
        return lax.rem(me + n - k, n)

    def owner_only(index, fn):
        if owners == n:
            fn()
        else:
            pl.when(index < owners)(fn)

    barrier = pltpu.get_barrier_semaphore()
    for k in range(1, n):
        pl.semaphore_signal(barrier, inc=1, device_id={"scan": peer(k)}, device_id_type=MESH)
    pl.semaphore_signal(barrier, inc=1, device_id=partner, device_id_type=MESH)
    for k in range(1, n):
        pl.semaphore_signal(
            barrier, inc=1, device_id={"scan": peer(k), **partner}, device_id_type=MESH
        )
    positions = load.shape[1]
    chunks = positions // pos_chunk
    num_copies = [
        remote(num_out.at[i], num_in.at[i], nm_sem.at[0, i], nm_sem.at[1, i], partner)
        for i in range(chunks)
    ]

    def products(i):
        part = pl.ds(i * pos_chunk, pos_chunk)
        both = dot_nt(s_hi[part, :], tied2[...])
        low = dot_nt(s_lo[part, :], tied2[:rank, :])
        num_out[i] = (both[:, :rank] + (both[:, rank:] + low)).T

    def update(i):
        num_copies[i].wait()
        cols = slice(i * pos_chunk, (i + 1) * pos_chunk)
        fresh = load[:, cols] * (num_out[i] + num_in[i]) / weighted[:, cols]
        new_loadings[:, cols] = fresh
        hi, lo = split(fresh)
        nl2[:rank, cols] = hi
        nl2[rank:, cols] = lo

    for i in range(chunks):
        products(i)
        if i == wait_at:
            pl.semaphore_wait(barrier, 2 * n - 1)
            for j in range(i):
                num_copies[j].start()
        if i >= wait_at:
            num_copies[i].start()
    for i in range(chunks):
        update(i)

    def sums(cols):
        both = dot_nn(nl2[...], s_hi[:, cols])
        low = dot_nn(nl2[:rank, :], s_lo[:, cols])
        return both[:rank] + (both[rank:] + low)

    step = col_chunk // LANES
    count = half // step
    w_copies = []
    for i in range(count):
        part = pl.ds(i * step, step)
        w_copies.append(
            remote(w_out.at[part], w_in.at[part], w_sem.at[0, i], w_sem.at[1, i], partner)
        )
    cr_copies = [None]
    for k in range(1, n):
        cr_copies.append(
            remote(cr_out, cr_in.at[k], cr_send.at[k], cr_recv.at[k], {"scan": peer(k)})
        )
    for i in range(count):
        first = half + i * step
        value = sums(slice(first * LANES, (first + step) * LANES))
        for j in range(step):
            w_out[i * step + j] = value[:, j * LANES:(j + 1) * LANES]
        w_copies[i].start()
    squares = dot_nt(nl2[...], nl2[...])
    cross = squares[:rank, :rank] + (squares[:rank, rank:] + squares[rank:, :rank])
    cr_out[...] = jnp.concatenate(
        [cross[i * (rank // pack):(i + 1) * (rank // pack)] for i in range(pack)], axis=1
    )
    for k in range(1, n):
        cr_copies[k].start()

    for i in range(count):
        value = sums(slice(i * col_chunk, (i + 1) * col_chunk))
        for j in range(step):
            w_keep[i * step + j] = value[:, j * LANES:(j + 1) * LANES]
    for copy in w_copies:
        copy.wait()
    for b in range(half):
        w_keep[b] = w_keep[b] + mirrored(w_in[half - 1 - b])

    rs_copies = [None]
    for k in range(1, n):
        rs_copies.append(
            remote(
                w_keep.at[piece_at(peer(k), per, row_split, rows)], rs_in.at[k],
                rs_send.at[k], rs_recv.at[k], {"scan": peer(k)},
            )
        )
        owner_only(peer(k), rs_copies[k].start)

    for k in range(1, n):
        cr_copies[k].wait()
    total = cr_out[...]
    for k in range(1, n):
        total = total + cr_in[k]
    cross = jnp.concatenate(
        [total[:, i * rank:(i + 1) * rank] for i in range(pack)], axis=0
    )

    ag_copies = [None]
    for k in range(1, n):
        ag_copies.append(
            remote(piece_buf, ag_in.at[k], ag_send.at[k], ag_recv.at[k], {"scan": peer(k)})
        )
    fw_copies = [remote(piece_buf, fw_in.at[0], fw_send.at[0], fw_recv.at[0], partner)]
    for k in range(1, n):
        fw_copies.append(
            remote(
                piece_buf, fw_in.at[k], fw_send.at[k], fw_recv.at[k],
                {"scan": peer(k), **partner},
            )
        )

    def own_piece():
        first, row = piece_at(me, per, row_split, rows)
        for j in range(per):
            weights = jnp.dot(
                cross, tied3[first.start + j], precision=HIGHEST, preferred_element_type=F32
            )
            if row_split > 1:
                piece_buf[0] = weights[:rows]
                for i in range(1, row_split):
                    @pl.when(lax.rem(me, row_split) == i)
                    def _():
                        piece_buf[0] = weights[i * rows:(i + 1) * rows]
            else:
                piece_buf[j] = weights
        for k in range(1, n):
            rs_copies[k].wait_recv()
        for j in range(per):
            total = w_keep[first.start + j, row, :]
            for k in range(1, n):
                total = total + rs_in[k, j]
            piece_buf[j] = tied3[first.start + j, row, :] * (0.5 * total) / piece_buf[j]
        for k in range(1, n):
            ag_copies[k].start()
            fw_copies[k].start()
        fw_copies[0].start()

    owner_only(me, own_piece)

    def arrived(k):
        def go():
            ag_copies[k].wait_recv()
        return go

    for k in range(1, n):
        owner_only(source(k), arrived(k))
    owner_only(me, fw_copies[0].wait)
    for k in range(1, n):
        owner_only(source(k), fw_copies[k].wait_recv)
    for k in range(1, n):
        owner_only(peer(k), rs_copies[k].wait_send)
        owner_only(me, ag_copies[k].wait_send)
        owner_only(me, fw_copies[k].wait_send)


def output_kernel(
    n, fresh, piece_buf, ag_in, fw_in, new_loadings, new_basis, nb, io_sem
):
    rank, pixels = nb.shape
    half, per, row_split = layout(n, rank, pixels)
    owners = half // per * row_split
    rows = rank // row_split
    me = lax.axis_index("scan")
    first_copy = pltpu.make_async_copy(fresh, new_loadings, io_sem.at[0])
    first_copy.start()

    def put(index, ref, flip):
        first, row = piece_at(index, per, row_split, rows)
        for j in range(per):
            block = first.start + j
            value = ref[j]
            if flip:
                block = pixels // LANES - 1 - block
                value = mirrored(value)
            nb[row, pl.ds(pl.multiple_of(block * LANES, LANES), LANES)] = value

    for k in range(n):
        index = lax.rem(me + n - k, n)

        def go():
            put(index, piece_buf if k == 0 else ag_in.at[k], False)
            put(index, fw_in.at[k], True)

        if owners == n:
            go()
        else:
            pl.when(index < owners)(go)
    second_copy = pltpu.make_async_copy(nb, new_basis, io_sem.at[1])
    second_copy.start()
    first_copy.wait()
    second_copy.wait()


def per_device(n, spectra, basis, loadings):
    rank, pixels = basis.shape
    positions = loadings.shape[1]
    blocks = pixels // LANES
    half, per, row_split = layout(n, rank, pixels)
    rows = rank // row_split
    load_chunks = 8
    pos_chunk = positions // 2
    col_chunk = 8 * LANES
    pack = LANES // rank
    dma = pltpu.SemaphoreType.DMA
    any_space = pl.BlockSpec(memory_space=pl.ANY)
    vmem = pl.BlockSpec(memory_space=pltpu.VMEM)
    hbm = pl.BlockSpec(memory_space=pltpu.HBM)
    inputs = [pltpu.with_memory_space_constraint(x, pltpu.HBM) for x in (spectra, basis, loadings)]
    parts = pl.pallas_call(
        functools.partial(tie_kernel, load_chunks, 6),
        out_shape=(
            pltpu.VMEM(spectra.shape, BF16),
            pltpu.VMEM(spectra.shape, BF16),
            pltpu.VMEM((blocks, rank, LANES), F32),
            pltpu.VMEM((2 * rank, pixels), BF16),
            pltpu.VMEM((rank, positions), F32),
            pltpu.VMEM((rank, positions), F32),
        ),
        in_specs=[hbm] * 3,
        out_specs=(vmem,) * 6,
        scratch_shapes=[
            pltpu.VMEM(spectra.shape, F32),
            pltpu.VMEM((rank, pixels), F32),
            pltpu.VMEM((rank, pixels), F32),
            dma((load_chunks,)),
            dma((2,)),
            dma((2,)),
        ],
        compiler_params=pltpu.CompilerParams(
            collective_id=0, has_side_effects=True, vmem_limit_bytes=32 << 20
        ),
        name="tie_and_split",
    )(*inputs)
    outs = pl.pallas_call(
        functools.partial(update_kernel, n, pos_chunk, col_chunk, 1),
        out_shape=(
            pltpu.VMEM(loadings.shape, F32),
            pltpu.VMEM((per, rows, LANES), F32),
            pltpu.VMEM((n, per, rows, LANES), F32),
            pltpu.VMEM((n, per, rows, LANES), F32),
        ),
        in_specs=[vmem] * 6,
        out_specs=(vmem,) * 4,
        scratch_shapes=[
            pltpu.VMEM((2 * rank, positions), BF16),
            pltpu.VMEM((positions // pos_chunk, rank, pos_chunk), F32),
            pltpu.VMEM((positions // pos_chunk, rank, pos_chunk), F32),
            pltpu.VMEM((half, rank, LANES), F32),
            pltpu.VMEM((half, rank, LANES), F32),
            pltpu.VMEM((half, rank, LANES), F32),
            pltpu.VMEM((n, per, rows, LANES), F32),
            pltpu.VMEM((rank // pack, LANES), F32),
            pltpu.VMEM((n, rank // pack, LANES), F32),
            dma((2, positions // pos_chunk)),
            dma((2, half * LANES // col_chunk)),
            dma((n,)), dma((n,)), dma((n,)), dma((n,)),
            dma((n,)), dma((n,)), dma((n,)), dma((n,)),
        ],
        compiler_params=pltpu.CompilerParams(
            collective_id=1, has_side_effects=True, vmem_limit_bytes=32 << 20
        ),
        name="update",
    )(*parts)
    return pl.pallas_call(
        functools.partial(output_kernel, n),
        out_shape=(
            jax.ShapeDtypeStruct(loadings.shape, F32),
            jax.ShapeDtypeStruct(basis.shape, F32),
        ),
        in_specs=[vmem] * 4,
        out_specs=(any_space,) * 2,
        scratch_shapes=[pltpu.VMEM((rank, pixels), F32), dma((2,))],
        compiler_params=pltpu.CompilerParams(vmem_limit_bytes=8 << 20),
        name="write_out",
    )(*outs)


def solution(mesh):
    in_specs = (P(("grp", "scan"), "det"), P("grp", "det"), P("grp", "scan"))
    out_specs = (P("grp", "scan"), P("grp", "det"))
    return jax.shard_map(
        functools.partial(per_device, mesh.shape["scan"]),
        mesh=mesh, in_specs=in_specs, out_specs=out_specs, check_vma=False,
    )
```

profile of v0, /device:TPU:0, one launch (start us, length us, event | category | flops | bytes accessed | tf_op | source)
XLA Modules:
  0.0 25.8 jit_solution(16694446272930369791)
XLA Ops:
  0.6 4.1 %tie_and_split.1 = (bf16[1024,2048]{1,0:T(8,128)(2,1)S(1)}, bf16[1024,2048]{1,0:T(8,128)(2,1)S(1)}, f32[16,32,128]{2,1,0:T(8,128)S(1)}, bf16[64,2048]{1,0:T(8,12...) custom-call(f32[1024,2048]{1,0:T(8,128)} %spectra.1, f32[32,2048]{1,0:T(8,128)} %basis.1, f32[32,1024]{1,0:T(8,128)} %loadings.1), custom_call_target="tpu_custom_call" | custom-call | tf_op jit(solution)/shard_map/tie_and_split/pallas_call | solution.py:364
  4.8 20.2 %update.1 = (f32[32,1024]{1,0:T(8,128)S(1)}, f32[1,32,128]{2,1,0:T(8,128)S(1)}, f32[8,1,32,128]{3,2,1,0:T(8,128)S(1)}, f32[8,1,32,128]{3,2,1,0:T(8,128)S(1)}) custom-call(bf16[1024,2048]{1,0:T(8,128)(2,1)S(1)} %get-tuple-element.12.s_hi, bf16[1024,2048]{1,0:T(8,128)(2,1)S(1)} %get-tuple-element.13.s_lo, f32[16,32,128]{2,1,0:T(8,128)S(1)} %get-tuple-element.14.tied3, ...), custom_call_target="tpu_custom_call" | custom-call | tf_op jit(solution)/shard_map/update/pallas_call | solution.py:389
  25.0 0.8 %write_out.1 = (f32[32,1024]{1,0:T(8,128)}, f32[32,2048]{1,0:T(8,128)}) custom-call(f32[32,1024]{1,0:T(8,128)S(1)} %get-tuple-element.18.fresh, f32[1,32,128]{2,1,0:T(8,128)S(1)} %get-tuple-element.19.piece_buf, f32[8,1,32,128]{3,2,1,0:T(8,128)S(1)} %get-tuple-element.20.ag_in, f32[8,1,32,128]{3,2,1,0:T(8,128)S(1)} %get-tuple-element.21.fw_in), custom_call_target="tpu_custom_call" | custom-call | tf_op jit(solution)/shard_map/write_out/pallas_call | solution.py:419
where the time goes:
time: 26 us; the launch traced here: 25.8 us
  Pallas kernels  25.2 us (97%)
  between operations  0.65 us (2%)
    pallas_call x1, Pallas kernels, per_device(): pl.pallas_call(functools.partial(update_kernel, n, pos_chunk, col_chunk,...  20.2 us
    pallas_call x1, Pallas kernels, per_device(): pl.pallas_call(functools.partial(tie_kernel, load_chunks, 6), out_shape=(...  4.13 us
    pallas_call x1, Pallas kernels, per_device(): pl.pallas_call(functools.partial(output_kernel, n), out_shape=(jax.ShapeD...  0.83 us

commit v1 on v0

--- a/solution.py
+++ b/solution.py
@@ -55,23 +55,31 @@
     return pl.ds(first, per), pl.ds(row, rows)
 
 
+def divide(source, s_hi, s_lo, start, rows):
+    @pl.loop(0, rows // 16, unroll=True)
+    def _(j):
+        part = pl.ds(pl.multiple_of(start + j * 16, 16), 16)
+        hi, lo = split(source[part, :])
+        s_hi[part, :] = hi
+        s_lo[part, :] = lo
+
+
 def tie_kernel(
-    load_chunks, early,
+    chunk, early,
     spectra, basis, loadings,
-    s_hi, s_lo, tied3, tied2, load, weighted,
+    s_hi, s_lo, tied3, tied2, load,
     sbuf, own, other, sp_sem, io_sem, bs_sem,
 ):
     rank, pixels = basis.shape
-    positions = loadings.shape[1]
     blocks = pixels // LANES
+    chunks = s_hi.shape[0] // chunk
     partner = {"det": 1 - lax.axis_index("det")}
     barrier = pltpu.get_barrier_semaphore()
     pl.semaphore_signal(barrier, inc=1, device_id=partner, device_id_type=MESH)
 
-    load_rows = positions // load_chunks
     spectra_copies = []
-    for i in range(load_chunks):
-        part = pl.ds(i * load_rows, load_rows)
+    for i in range(chunks):
+        part = pl.ds(i * chunk, chunk)
         spectra_copies.append(
             pltpu.make_async_copy(spectra.at[part], sbuf.at[part], sp_sem.at[i])
         )
@@ -83,22 +91,13 @@
     pl.semaphore_wait(barrier, 1)
     basis_copy.start()
     own_copy.start()
+    for i in range(early, chunks):
+        spectra_copies[i].start()
     load_copy.start()
-    for i in range(early, load_chunks):
-        spectra_copies[i].start()
-
-    def divide(i):
+
+    for i in range(chunks - 1):
         spectra_copies[i].wait()
-
-        @pl.loop(0, load_rows // 16, unroll=True)
-        def _(j):
-            part = pl.ds(pl.multiple_of(i * load_rows + j * 16, 16), 16)
-            hi, lo = split(sbuf[part, :])
-            s_hi[part, :] = hi
-            s_lo[part, :] = lo
-
-    for i in range(early):
-        divide(i)
+        divide(sbuf, s_hi, s_lo, i * chunk, chunk)
     own_copy.wait()
     basis_copy.wait()
     for b in range(blocks):
@@ -109,24 +108,18 @@
         hi, lo = split(tied)
         tied2[:rank, b * LANES:(b + 1) * LANES] = hi
         tied2[rank:, b * LANES:(b + 1) * LANES] = lo
-    squares = dot_nt(tied2[...], tied2[...])
-    gram = 2.0 * (
-        squares[:rank, :rank] + (squares[:rank, rank:] + squares[rank:, :rank])
-    )
+    spectra_copies[chunks - 1].wait()
+    divide(sbuf, s_hi, s_lo, (chunks - 1) * chunk, chunk)
     load_copy.wait()
-    weighted[...] = jnp.dot(
-        gram, load[...], precision=HIGHEST, preferred_element_type=F32
-    )
-    for i in range(early, load_chunks):
-        divide(i)
 
 
 def update_kernel(
-    n, pos_chunk, col_chunk, wait_at,
-    s_hi, s_lo, tied3, tied2, load, weighted,
-    new_loadings, piece_buf, ag_in, fw_in,
+    n, chunk, pos_chunk, col_chunk, wait_at,
+    spectra, a_hi, a_lo, tied3, tied2, load,
+    new_loadings, ag_in, fw_in,
+    sbuf, b_hi, b_lo, weighted,
     nl2, num_out, num_in, w_keep, w_out, w_in, rs_in, cr_out, cr_in,
-    nm_sem, w_sem, rs_send, rs_recv, cr_send, cr_recv,
+    sp_sem, nm_sem, w_sem, rs_send, rs_recv, cr_send, cr_recv,
     ag_send, ag_recv, fw_send, fw_recv,
 ):
     blocks, rank, _ = tied3.shape
@@ -136,6 +129,8 @@
     pack = LANES // rank
     me = lax.axis_index("scan")
     partner = {"det": 1 - lax.axis_index("det")}
+    first_rows = a_hi.shape[0]
+    last_rows = b_hi.shape[0]
 
     def peer(k):
         return lax.rem(me + k, n)
@@ -149,14 +144,19 @@
         else:
             pl.when(index < owners)(fn)
 
+    spectra_copies = []
+    for i in range(last_rows // chunk):
+        spectra_copies.append(
+            pltpu.make_async_copy(
+                spectra.at[pl.ds(first_rows + i * chunk, chunk)],
+                sbuf.at[pl.ds(i * chunk, chunk)], sp_sem.at[i],
+            )
+        )
+        spectra_copies[i].start()
     barrier = pltpu.get_barrier_semaphore()
     for k in range(1, n):
         pl.semaphore_signal(barrier, inc=1, device_id={"scan": peer(k)}, device_id_type=MESH)
     pl.semaphore_signal(barrier, inc=1, device_id=partner, device_id_type=MESH)
-    for k in range(1, n):
-        pl.semaphore_signal(
-            barrier, inc=1, device_id={"scan": peer(k), **partner}, device_id_type=MESH
-        )
     positions = load.shape[1]
     chunks = positions // pos_chunk
     num_copies = [
@@ -164,13 +164,75 @@
         for i in range(chunks)
     ]
 
-    def products(i):
-        part = pl.ds(i * pos_chunk, pos_chunk)
-        both = dot_nt(s_hi[part, :], tied2[...])
-        low = dot_nt(s_lo[part, :], tied2[:rank, :])
-        num_out[i] = (both[:, :rank] + (both[:, rank:] + low)).T
-
-    def update(i):
+    def rows_of(start, size):
+        if start < first_rows:
+            return a_hi, a_lo, slice(start, start + size)
+        return b_hi, b_lo, slice(start - first_rows, start - first_rows + size)
+
+    def products(start):
+        hi_ref, lo_ref, part = rows_of(start, chunk)
+        both = dot_nt(hi_ref[part, :], tied2[...])
+        low = dot_nt(lo_ref[part, :], tied2[:rank, :])
+        at = start % pos_chunk
+        num_out[start // pos_chunk, :, at:at + chunk] = (
+            both[:, :rank] + (both[:, rank:] + low)
+        ).T
+
+    def send(i):
+        if i == wait_at:
+            pl.semaphore_wait(barrier, n)
+            for j in range(i):
+                num_copies[j].start()
+        if i >= wait_at:
+            num_copies[i].start()
+
+    squares = dot_nt(tied2[...], tied2[...])
+    gram = 2.0 * (
+        squares[:rank, :rank] + (squares[:rank, rank:] + squares[rank:, :rank])
+    )
+    weighted[...] = jnp.dot(
+        gram, load[...], precision=HIGHEST, preferred_element_type=F32
+    )
+    steps = positions // chunk
+    for i in range(steps):
+        later = (i + 1) * chunk - first_rows
+        if 0 <= later < last_rows:
+            spectra_copies[later // chunk].wait()
+            divide(sbuf, b_hi, b_lo, later, chunk)
+        products(i * chunk)
+        if (i + 1) * chunk % pos_chunk == 0:
+            send((i + 1) * chunk // pos_chunk - 1)
+
+    def sums(i, cols):
+        hi_ref, lo_ref, part = rows_of(i * pos_chunk, pos_chunk)
+        where = slice(i * pos_chunk, (i + 1) * pos_chunk)
+        both = dot_nn(nl2[:, where], hi_ref[part, cols])
+        low = dot_nn(nl2[:rank, where], lo_ref[part, cols])
+        return both[:rank] + (both[rank:] + low)
+
+    step = col_chunk // LANES
+    count = half // step
+
+    def accumulate(i, target, first):
+        for c in range(count):
+            start = first + c * step
+            value = sums(i, slice(start * LANES, (start + step) * LANES))
+            for j in range(step):
+                at = value[:, j * LANES:(j + 1) * LANES]
+                if i == 0:
+                    target[c * step + j] = at
+                else:
+                    target[c * step + j] = target[c * step + j] + at
+            if target is w_out and i == chunks - 1:
+                w_copies[c].start()
+
+    w_copies = []
+    for i in range(count):
+        part = pl.ds(i * step, step)
+        w_copies.append(
+            remote(w_out.at[part], w_in.at[part], w_sem.at[0, i], w_sem.at[1, i], partner)
+        )
+    for i in range(chunks):
         num_copies[i].wait()
         cols = slice(i * pos_chunk, (i + 1) * pos_chunk)
         fresh = load[:, cols] * (num_out[i] + num_in[i]) / weighted[:, cols]
@@ -178,42 +240,14 @@
         hi, lo = split(fresh)
         nl2[:rank, cols] = hi
         nl2[rank:, cols] = lo
-
-    for i in range(chunks):
-        products(i)
-        if i == wait_at:
-            pl.semaphore_wait(barrier, 2 * n - 1)
-            for j in range(i):
-                num_copies[j].start()
-        if i >= wait_at:
-            num_copies[i].start()
-    for i in range(chunks):
-        update(i)
-
-    def sums(cols):
-        both = dot_nn(nl2[...], s_hi[:, cols])
-        low = dot_nn(nl2[:rank, :], s_lo[:, cols])
-        return both[:rank] + (both[rank:] + low)
-
-    step = col_chunk // LANES
-    count = half // step
-    w_copies = []
-    for i in range(count):
-        part = pl.ds(i * step, step)
-        w_copies.append(
-            remote(w_out.at[part], w_in.at[part], w_sem.at[0, i], w_sem.at[1, i], partner)
-        )
+        accumulate(i, w_out, half)
+        if i < chunks - 1:
+            accumulate(i, w_keep, 0)
     cr_copies = [None]
     for k in range(1, n):
         cr_copies.append(
             remote(cr_out, cr_in.at[k], cr_send.at[k], cr_recv.at[k], {"scan": peer(k)})
         )
-    for i in range(count):
-        first = half + i * step
-        value = sums(slice(first * LANES, (first + step) * LANES))
-        for j in range(step):
-            w_out[i * step + j] = value[:, j * LANES:(j + 1) * LANES]
-        w_copies[i].start()
     squares = dot_nt(nl2[...], nl2[...])
     cross = squares[:rank, :rank] + (squares[:rank, rank:] + squares[rank:, :rank])
     cr_out[...] = jnp.concatenate(
@@ -222,10 +256,7 @@
     for k in range(1, n):
         cr_copies[k].start()
 
-    for i in range(count):
-        value = sums(slice(i * col_chunk, (i + 1) * col_chunk))
-        for j in range(step):
-            w_keep[i * step + j] = value[:, j * LANES:(j + 1) * LANES]
+    accumulate(chunks - 1, w_keep, 0)
     for copy in w_copies:
         copy.wait()
     for b in range(half):
@@ -242,7 +273,7 @@
         owner_only(peer(k), rs_copies[k].start)
 
     for k in range(1, n):
-        cr_copies[k].wait()
+        cr_copies[k].wait_recv()
     total = cr_out[...]
     for k in range(1, n):
         total = total + cr_in[k]
@@ -250,19 +281,19 @@
         [total[:, i * rank:(i + 1) * rank] for i in range(pack)], axis=0
     )
 
+    piece_buf = ag_in.at[0]
     ag_copies = [None]
     for k in range(1, n):
         ag_copies.append(
             remote(piece_buf, ag_in.at[k], ag_send.at[k], ag_recv.at[k], {"scan": peer(k)})
         )
-    fw_copies = [remote(piece_buf, fw_in.at[0], fw_send.at[0], fw_recv.at[0], partner)]
-    for k in range(1, n):
-        fw_copies.append(
-            remote(
-                piece_buf, fw_in.at[k], fw_send.at[k], fw_recv.at[k],
-                {"scan": peer(k), **partner},
-            )
-        )
+    if owners == n:
+        fw_copies = [remote(ag_in, fw_in, fw_send.at[0], fw_recv.at[0], partner)]
+    else:
+        fw_copies = [
+            remote(ag_in.at[k], fw_in.at[k], fw_send.at[k], fw_recv.at[k], partner)
+            for k in range(n)
+        ]
 
     def own_piece():
         first, row = piece_at(me, per, row_split, rows)
@@ -287,29 +318,32 @@
             piece_buf[j] = tied3[first.start + j, row, :] * (0.5 * total) / piece_buf[j]
         for k in range(1, n):
             ag_copies[k].start()
-            fw_copies[k].start()
-        fw_copies[0].start()
+        if owners < n:
+            fw_copies[0].start()
 
     owner_only(me, own_piece)
 
     def arrived(k):
         def go():
             ag_copies[k].wait_recv()
+            if owners < n:
+                fw_copies[k].start()
         return go
 
     for k in range(1, n):
         owner_only(source(k), arrived(k))
-    owner_only(me, fw_copies[0].wait)
-    for k in range(1, n):
-        owner_only(source(k), fw_copies[k].wait_recv)
-    for k in range(1, n):
+    if owners == n:
+        fw_copies[0].start()
+    for k in range(1, n):
+        cr_copies[k].wait_send()
         owner_only(peer(k), rs_copies[k].wait_send)
         owner_only(me, ag_copies[k].wait_send)
-        owner_only(me, fw_copies[k].wait_send)
+    for k, copy in enumerate(fw_copies):
+        owner_only(source(k), copy.wait)
 
 
 def output_kernel(
-    n, fresh, piece_buf, ag_in, fw_in, new_loadings, new_basis, nb, io_sem
+    n, fresh, ag_in, fw_in, new_loadings, new_basis, nb, io_sem
 ):
     rank, pixels = nb.shape
     half, per, row_split = layout(n, rank, pixels)
@@ -333,7 +367,7 @@
         index = lax.rem(me + n - k, n)
 
         def go():
-            put(index, piece_buf if k == 0 else ag_in.at[k], False)
+            put(index, ag_in.at[k], False)
             put(index, fw_in.at[k], True)
 
         if owners == n:
@@ -352,9 +386,11 @@
     blocks = pixels // LANES
     half, per, row_split = layout(n, rank, pixels)
     rows = rank // row_split
-    load_chunks = 8
-    pos_chunk = positions // 2
-    col_chunk = 8 * LANES
+    chunk = positions // 8
+    first_rows = positions // 2
+    last_rows = positions - first_rows
+    pos_chunk = positions // 4
+    col_chunk = 4 * LANES
     pack = LANES // rank
     dma = pltpu.SemaphoreType.DMA
     any_space = pl.BlockSpec(memory_space=pl.ANY)
@@ -362,22 +398,21 @@
     hbm = pl.BlockSpec(memory_space=pltpu.HBM)
     inputs = [pltpu.with_memory_space_constraint(x, pltpu.HBM) for x in (spectra, basis, loadings)]
     parts = pl.pallas_call(
-        functools.partial(tie_kernel, load_chunks, 6),
+        functools.partial(tie_kernel, chunk, 2),
         out_shape=(
-            pltpu.VMEM(spectra.shape, BF16),
-            pltpu.VMEM(spectra.shape, BF16),
+            pltpu.VMEM((first_rows, pixels), BF16),
+            pltpu.VMEM((first_rows, pixels), BF16),
             pltpu.VMEM((blocks, rank, LANES), F32),
             pltpu.VMEM((2 * rank, pixels), BF16),
             pltpu.VMEM((rank, positions), F32),
-            pltpu.VMEM((rank, positions), F32),
         ),
         in_specs=[hbm] * 3,
-        out_specs=(vmem,) * 6,
+        out_specs=(vmem,) * 5,
         scratch_shapes=[
-            pltpu.VMEM(spectra.shape, F32),
+            pltpu.VMEM((first_rows, pixels), F32),
             pltpu.VMEM((rank, pixels), F32),
             pltpu.VMEM((rank, pixels), F32),
-            dma((load_chunks,)),
+            dma((first_rows // chunk,)),
             dma((2,)),
             dma((2,)),
         ],
@@ -387,16 +422,19 @@
         name="tie_and_split",
     )(*inputs)
     outs = pl.pallas_call(
-        functools.partial(update_kernel, n, pos_chunk, col_chunk, 1),
+        functools.partial(update_kernel, n, chunk, pos_chunk, col_chunk, 2),
         out_shape=(
             pltpu.VMEM(loadings.shape, F32),
-            pltpu.VMEM((per, rows, LANES), F32),
             pltpu.VMEM((n, per, rows, LANES), F32),
             pltpu.VMEM((n, per, rows, LANES), F32),
         ),
-        in_specs=[vmem] * 6,
-        out_specs=(vmem,) * 4,
+        in_specs=[hbm] + [vmem] * 5,
+        out_specs=(vmem,) * 3,
         scratch_shapes=[
+            pltpu.VMEM((last_rows, pixels), F32),
+            pltpu.VMEM((last_rows, pixels), BF16),
+            pltpu.VMEM((last_rows, pixels), BF16),
+            pltpu.VMEM((rank, positions), F32),
             pltpu.VMEM((2 * rank, positions), BF16),
             pltpu.VMEM((positions // pos_chunk, rank, pos_chunk), F32),
             pltpu.VMEM((positions // pos_chunk, rank, pos_chunk), F32),
@@ -406,23 +444,24 @@
             pltpu.VMEM((n, per, rows, LANES), F32),
             pltpu.VMEM((rank // pack, LANES), F32),
             pltpu.VMEM((n, rank // pack, LANES), F32),
+            dma((last_rows // chunk,)),
             dma((2, positions // pos_chunk)),
             dma((2, half * LANES // col_chunk)),
             dma((n,)), dma((n,)), dma((n,)), dma((n,)),
             dma((n,)), dma((n,)), dma((n,)), dma((n,)),
         ],
         compiler_params=pltpu.CompilerParams(
-            collective_id=1, has_side_effects=True, vmem_limit_bytes=32 << 20
+            collective_id=1, has_side_effects=True, vmem_limit_bytes=40 << 20
         ),
         name="update",
-    )(*parts)
+    )(inputs[0], *parts)
     return pl.pallas_call(
         functools.partial(output_kernel, n),
         out_shape=(
             jax.ShapeDtypeStruct(loadings.shape, F32),
             jax.ShapeDtypeStruct(basis.shape, F32),
         ),
-        in_specs=[vmem] * 4,
+        in_specs=[vmem] * 3,
         out_specs=(any_space,) * 2,
         scratch_shapes=[pltpu.VMEM((rank, pixels), F32), dma((2,))],
         compiler_params=pltpu.CompilerParams(vmem_limit_bytes=8 << 20),

time: 26 us -> 25.4 us (0.977)
  Pallas kernels: 25.2 us -> 24.6 us
    pallas_call x2, Pallas kernels: 24.4 us -> 23.8 us  [the longest x1 21.2 us: per_device(): pl.pallas_call(functools.partial(update_kernel, n, chunk, pos_chunk, col_...]
where the time goes in v1:
time: 25.4 us; the launch traced here: 25.2 us
  Pallas kernels  24.6 us (97%)
  between operations  0.65 us (3%)
    pallas_call x1, Pallas kernels, per_device(): pl.pallas_call(functools.partial(update_kernel, n, chunk, pos_chunk, col_...  21.2 us
    pallas_call x1, Pallas kernels, per_device(): pl.pallas_call(functools.partial(tie_kernel, chunk, 2), out_shape=(pltpu....  2.61 us
    pallas_call x1, Pallas kernels, per_device(): pl.pallas_call(functools.partial(output_kernel, n), out_shape=(jax.ShapeD...  0.83 us

profile of v1, /device:TPU:0, one launch (start us, length us, event | category | flops | bytes accessed | tf_op | source)
XLA Modules:
  0.0 25.2 jit_solution(6433543186747482993)
XLA Ops:
  0.6 2.6 %tie_and_split.1 = (bf16[512,2048]{1,0:T(8,128)(2,1)S(1)}, bf16[512,2048]{1,0:T(8,128)(2,1)S(1)}, f32[16,32,128]{2,1,0:T(8,128)S(1)}, bf16[64,2048]{1,0:T(8,128)(2,1)S(1)}, f32[32,1024]{1,0:T(8,128)S(1)}) custom-call(f32[1024,2048]{1,0:T(8,128)} %spectra.3, f32[32,2048]{1,0:T(8,128)} %basis.1, f32[32,1024]{1,0:T(8,128)} %loadings.1), custom_call_target="tpu_custom_call" | custom-call | tf_op jit(solution)/shard_map/tie_and_split/pallas_call | solution.py:400
  3.2 21.2 %update.1 = (f32[32,1024]{1,0:T(8,128)S(1)}, f32[8,1,32,128]{3,2,1,0:T(8,128)S(1)}, f32[8,1,32,128]{3,2,1,0:T(8,128)S(1)}) custom-call(f32[1024,2048]{1,0:T(8,128)} %spectra.3, bf16[512,2048]{1,0:T(8,128)(2,1)S(1)} %get-tuple-element.10.a_hi, bf16[512,2048]{1,0:T(8,128)(2,1)S(1)} %get-tuple-element.11.a_lo, f32[16,32,128]{2,1,0:T(8,128)S(1)} %get-tuple-element.12.tied3, ...), custom_call_target="tpu_custom_call" | custom-call | tf_op jit(solution)/shard_map/update/pallas_call | solution.py:424
  24.4 0.8 %write_out.1 = (f32[32,1024]{1,0:T(8,128)}, f32[32,2048]{1,0:T(8,128)}) custom-call(f32[32,1024]{1,0:T(8,128)S(1)} %get-tuple-element.15.fresh, f32[8,1,32,128]{3,2,1,0:T(8,128)S(1)} %get-tuple-element.16.ag_in, f32[8,1,32,128]{3,2,1,0:T(8,128)S(1)} %get-tuple-element.17.fw_in), custom_call_target="tpu_custom_call" | custom-call | tf_op jit(solution)/shard_map/write_out/pallas_call | solution.py:458

commit v2 on v1

--- a/solution.py
+++ b/solution.py
@@ -64,21 +64,47 @@
         s_lo[part, :] = lo
 
 
-def tie_kernel(
-    chunk, early,
+def update_kernel(
+    n, chunk, early, pos_chunk, col_chunk,
     spectra, basis, loadings,
-    s_hi, s_lo, tied3, tied2, load,
-    sbuf, own, other, sp_sem, io_sem, bs_sem,
+    new_loadings, ag_in, fw_in,
+    sbuf, s_hi, s_lo, own, other, tied3, tied2, load, weighted,
+    nl2, num_out, num_in, w_keep, w_out, w_in, rs_in, cr_out, cr_in,
+    hello, ready, sp_sem, io_sem, bs_sem,
+    nm_sem, w_sem, rs_send, rs_recv, cr_send, cr_recv,
+    ag_send, ag_recv, fw_send, fw_recv,
 ):
-    rank, pixels = basis.shape
-    blocks = pixels // LANES
-    chunks = s_hi.shape[0] // chunk
-    partner = {"det": 1 - lax.axis_index("det")}
+    blocks, rank, _ = tied3.shape
+    half, per, row_split = layout(n, rank, blocks * LANES)
+    owners = half // per * row_split
+    rows = rank // row_split
+    pack = LANES // rank
+    me = lax.axis_index("scan")
+    det = lax.axis_index("det")
+    partner = {"det": 1 - det}
+    positions = load.shape[1]
+    first_rows = positions // 2
+
+    def peer(k):
+        return lax.rem(me + k, n)
+
+    def source(k):
+        return lax.rem(me + n - k, n)
+
+    def owner_only(index, fn):
+        if owners == n:
+            fn()
+        else:
+            pl.when(index < owners)(fn)
+
     barrier = pltpu.get_barrier_semaphore()
-    pl.semaphore_signal(barrier, inc=1, device_id=partner, device_id_type=MESH)
+
+    @pl.when(det == 0)
+    def _():
+        pl.semaphore_signal(barrier, inc=1, device_id=partner, device_id_type=MESH)
 
     spectra_copies = []
-    for i in range(chunks):
+    for i in range(positions // chunk):
         part = pl.ds(i * chunk, chunk)
         spectra_copies.append(
             pltpu.make_async_copy(spectra.at[part], sbuf.at[part], sp_sem.at[i])
@@ -88,18 +114,33 @@
     basis_copy = remote(basis, other, bs_sem.at[0], bs_sem.at[1], partner)
     for i in range(early):
         spectra_copies[i].start()
-    pl.semaphore_wait(barrier, 1)
-    basis_copy.start()
+
+    @pl.when(det == 1)
+    def _():
+        pl.semaphore_wait(barrier, 1)
+        pl.semaphore_signal(hello, inc=1, device_id=partner, device_id_type=MESH)
+        basis_copy.start()
+
+    @pl.when(det == 0)
+    def _():
+        pl.semaphore_wait(hello, 1)
+        basis_copy.start()
+        for k in range(1, n):
+            pl.semaphore_signal(
+                barrier, inc=1, device_id={"scan": peer(k)}, device_id_type=MESH
+            )
+
     own_copy.start()
-    for i in range(early, chunks):
+    for i in range(early, len(spectra_copies)):
         spectra_copies[i].start()
     load_copy.start()
 
-    for i in range(chunks - 1):
+    first_chunks = first_rows // chunk
+    for i in range(first_chunks):
         spectra_copies[i].wait()
         divide(sbuf, s_hi, s_lo, i * chunk, chunk)
     own_copy.wait()
-    basis_copy.wait()
+    basis_copy.wait_recv()
     for b in range(blocks):
         mine = own[:, b * LANES:(b + 1) * LANES]
         back = blocks - 1 - b
@@ -108,84 +149,25 @@
         hi, lo = split(tied)
         tied2[:rank, b * LANES:(b + 1) * LANES] = hi
         tied2[rank:, b * LANES:(b + 1) * LANES] = lo
-    spectra_copies[chunks - 1].wait()
-    divide(sbuf, s_hi, s_lo, (chunks - 1) * chunk, chunk)
     load_copy.wait()
 
-
-def update_kernel(
-    n, chunk, pos_chunk, col_chunk, wait_at,
-    spectra, a_hi, a_lo, tied3, tied2, load,
-    new_loadings, ag_in, fw_in,
-    sbuf, b_hi, b_lo, weighted,
-    nl2, num_out, num_in, w_keep, w_out, w_in, rs_in, cr_out, cr_in,
-    sp_sem, nm_sem, w_sem, rs_send, rs_recv, cr_send, cr_recv,
-    ag_send, ag_recv, fw_send, fw_recv,
-):
-    blocks, rank, _ = tied3.shape
-    half, per, row_split = layout(n, rank, blocks * LANES)
-    owners = half // per * row_split
-    rows = rank // row_split
-    pack = LANES // rank
-    me = lax.axis_index("scan")
-    partner = {"det": 1 - lax.axis_index("det")}
-    first_rows = a_hi.shape[0]
-    last_rows = b_hi.shape[0]
-
-    def peer(k):
-        return lax.rem(me + k, n)
-
-    def source(k):
-        return lax.rem(me + n - k, n)
-
-    def owner_only(index, fn):
-        if owners == n:
-            fn()
-        else:
-            pl.when(index < owners)(fn)
-
-    spectra_copies = []
-    for i in range(last_rows // chunk):
-        spectra_copies.append(
-            pltpu.make_async_copy(
-                spectra.at[pl.ds(first_rows + i * chunk, chunk)],
-                sbuf.at[pl.ds(i * chunk, chunk)], sp_sem.at[i],
-            )
-        )
-        spectra_copies[i].start()
-    barrier = pltpu.get_barrier_semaphore()
-    for k in range(1, n):
-        pl.semaphore_signal(barrier, inc=1, device_id={"scan": peer(k)}, device_id_type=MESH)
-    pl.semaphore_signal(barrier, inc=1, device_id=partner, device_id_type=MESH)
-    positions = load.shape[1]
     chunks = positions // pos_chunk
     num_copies = [
         remote(num_out.at[i], num_in.at[i], nm_sem.at[0, i], nm_sem.at[1, i], partner)
         for i in range(chunks)
     ]
 
-    def rows_of(start, size):
-        if start < first_rows:
-            return a_hi, a_lo, slice(start, start + size)
-        return b_hi, b_lo, slice(start - first_rows, start - first_rows + size)
-
     def products(start):
-        hi_ref, lo_ref, part = rows_of(start, chunk)
-        both = dot_nt(hi_ref[part, :], tied2[...])
-        low = dot_nt(lo_ref[part, :], tied2[:rank, :])
+        part = slice(start, start + chunk)
+        both = dot_nt(s_hi[part, :], tied2[...])
+        low = dot_nt(s_lo[part, :], tied2[:rank, :])
         at = start % pos_chunk
         num_out[start // pos_chunk, :, at:at + chunk] = (
             both[:, :rank] + (both[:, rank:] + low)
         ).T
 
-    def send(i):
-        if i == wait_at:
-            pl.semaphore_wait(barrier, n)
-            for j in range(i):
-                num_copies[j].start()
-        if i >= wait_at:
-            num_copies[i].start()
-
+    for i in range(first_chunks):
+        products(i * chunk)
     squares = dot_nt(tied2[...], tied2[...])
     gram = 2.0 * (
         squares[:rank, :rank] + (squares[:rank, rank:] + squares[rank:, :rank])
@@ -193,56 +175,71 @@
     weighted[...] = jnp.dot(
         gram, load[...], precision=HIGHEST, preferred_element_type=F32
     )
-    steps = positions // chunk
-    for i in range(steps):
-        later = (i + 1) * chunk - first_rows
-        if 0 <= later < last_rows:
-            spectra_copies[later // chunk].wait()
-            divide(sbuf, b_hi, b_lo, later, chunk)
+    for i in range(chunks // 2):
+        num_copies[i].start()
+    for copy in spectra_copies[first_chunks:]:
+        copy.wait()
+    divide(sbuf, s_hi, s_lo, first_rows, chunk)
+    for i in range(first_chunks, positions // chunk):
+        if (i + 1) * chunk < positions:
+            divide(sbuf, s_hi, s_lo, (i + 1) * chunk, chunk)
         products(i * chunk)
-        if (i + 1) * chunk % pos_chunk == 0:
-            send((i + 1) * chunk // pos_chunk - 1)
-
-    def sums(i, cols):
-        hi_ref, lo_ref, part = rows_of(i * pos_chunk, pos_chunk)
-        where = slice(i * pos_chunk, (i + 1) * pos_chunk)
-        both = dot_nn(nl2[:, where], hi_ref[part, cols])
-        low = dot_nn(nl2[:rank, where], lo_ref[part, cols])
-        return both[:rank] + (both[rank:] + low)
-
-    step = col_chunk // LANES
-    count = half // step
-
-    def accumulate(i, target, first):
-        for c in range(count):
-            start = first + c * step
-            value = sums(i, slice(start * LANES, (start + step) * LANES))
-            for j in range(step):
-                at = value[:, j * LANES:(j + 1) * LANES]
-                if i == 0:
-                    target[c * step + j] = at
-                else:
-                    target[c * step + j] = target[c * step + j] + at
-            if target is w_out and i == chunks - 1:
-                w_copies[c].start()
-
-    w_copies = []
-    for i in range(count):
-        part = pl.ds(i * step, step)
-        w_copies.append(
-            remote(w_out.at[part], w_in.at[part], w_sem.at[0, i], w_sem.at[1, i], partner)
-        )
-    for i in range(chunks):
-        num_copies[i].wait()
+    for i in range(chunks // 2, chunks):
+        num_copies[i].start()
+
+    def update(i):
+        num_copies[i].wait_recv()
         cols = slice(i * pos_chunk, (i + 1) * pos_chunk)
         fresh = load[:, cols] * (num_out[i] + num_in[i]) / weighted[:, cols]
         new_loadings[:, cols] = fresh
         hi, lo = split(fresh)
         nl2[:rank, cols] = hi
         nl2[rank:, cols] = lo
-        accumulate(i, w_out, half)
-        if i < chunks - 1:
-            accumulate(i, w_keep, 0)
+
+    def sums(cols, where):
+        both = dot_nn(nl2[:, where], s_hi[where, cols])
+        low = dot_nn(nl2[:rank, where], s_lo[where, cols])
+        return both[:rank] + (both[rank:] + low)
+
+    step = col_chunk // LANES
+    count = half // step
+
+    def accumulate(target, first, i, where, add):
+        start = first + i * step
+        value = sums(slice(start * LANES, (start + step) * LANES), where)
+        for j in range(step):
+            at = value[:, j * LANES:(j + 1) * LANES]
+            target[i * step + j] = target[i * step + j] + at if add else at
+
+    w_copies = []
+    for i in range(count):
+        part = pl.ds(i * step, step)
+        w_copies.append(
+            remote(w_out.at[part], w_in.at[part], w_sem.at[0, i], w_sem.at[1, i], partner)
+        )
+    early_rows, late_rows = slice(0, first_rows), slice(first_rows, positions)
+    for i in range(chunks // 2):
+        update(i)
+    for i in range(count):
+        accumulate(w_out, half, i, early_rows, False)
+    for i in range(count):
+        accumulate(w_keep, 0, i, early_rows, False)
+
+    @pl.when(det == 0)
+    def _():
+        pl.semaphore_wait(barrier, n - 1)
+        pl.semaphore_signal(ready, inc=1, device_id=partner, device_id_type=MESH)
+
+    for i in range(chunks // 2, chunks):
+        update(i)
+    for i in range(count):
+        accumulate(w_out, half, i, late_rows, True)
+        w_copies[i].start()
+
+    @pl.when(det == 1)
+    def _():
+        pl.semaphore_wait(ready, 1)
+
     cr_copies = [None]
     for k in range(1, n):
         cr_copies.append(
@@ -256,11 +253,8 @@
     for k in range(1, n):
         cr_copies[k].start()
 
-    accumulate(chunks - 1, w_keep, 0)
-    for copy in w_copies:
-        copy.wait()
-    for b in range(half):
-        w_keep[b] = w_keep[b] + mirrored(w_in[half - 1 - b])
+    for i in range(count):
+        accumulate(w_keep, 0, i, late_rows, True)
 
     rs_copies = [None]
     for k in range(1, n):
@@ -270,6 +264,12 @@
                 rs_send.at[k], rs_recv.at[k], {"scan": peer(k)},
             )
         )
+    for i in range(count):
+        w_copies[i].wait_recv()
+        for j in range(step):
+            b = half - 1 - (i * step + j)
+            w_keep[b] = w_keep[b] + mirrored(w_in[half - 1 - b])
+    for k in range(1, n):
         owner_only(peer(k), rs_copies[k].start)
 
     for k in range(1, n):
@@ -338,6 +338,8 @@
         cr_copies[k].wait_send()
         owner_only(peer(k), rs_copies[k].wait_send)
         owner_only(me, ag_copies[k].wait_send)
+    for copy in [basis_copy] + num_copies + w_copies:
+        copy.wait_send()
     for k, copy in enumerate(fw_copies):
         owner_only(source(k), copy.wait)
 
@@ -387,8 +389,6 @@
     half, per, row_split = layout(n, rank, pixels)
     rows = rank // row_split
     chunk = positions // 8
-    first_rows = positions // 2
-    last_rows = positions - first_rows
     pos_chunk = positions // 4
     col_chunk = 4 * LANES
     pack = LANES // rank
@@ -397,43 +397,24 @@
     vmem = pl.BlockSpec(memory_space=pltpu.VMEM)
     hbm = pl.BlockSpec(memory_space=pltpu.HBM)
     inputs = [pltpu.with_memory_space_constraint(x, pltpu.HBM) for x in (spectra, basis, loadings)]
-    parts = pl.pallas_call(
-        functools.partial(tie_kernel, chunk, 2),
-        out_shape=(
-            pltpu.VMEM((first_rows, pixels), BF16),
-            pltpu.VMEM((first_rows, pixels), BF16),
-            pltpu.VMEM((blocks, rank, LANES), F32),
-            pltpu.VMEM((2 * rank, pixels), BF16),
-            pltpu.VMEM((rank, positions), F32),
-        ),
-        in_specs=[hbm] * 3,
-        out_specs=(vmem,) * 5,
-        scratch_shapes=[
-            pltpu.VMEM((first_rows, pixels), F32),
-            pltpu.VMEM((rank, pixels), F32),
-            pltpu.VMEM((rank, pixels), F32),
-            dma((first_rows // chunk,)),
-            dma((2,)),
-            dma((2,)),
-        ],
-        compiler_params=pltpu.CompilerParams(
-            collective_id=0, has_side_effects=True, vmem_limit_bytes=32 << 20
-        ),
-        name="tie_and_split",
-    )(*inputs)
     outs = pl.pallas_call(
-        functools.partial(update_kernel, n, chunk, pos_chunk, col_chunk, 2),
+        functools.partial(update_kernel, n, chunk, 3, pos_chunk, col_chunk),
         out_shape=(
             pltpu.VMEM(loadings.shape, F32),
             pltpu.VMEM((n, per, rows, LANES), F32),
             pltpu.VMEM((n, per, rows, LANES), F32),
         ),
-        in_specs=[hbm] + [vmem] * 5,
+        in_specs=[hbm] * 3,
         out_specs=(vmem,) * 3,
         scratch_shapes=[
-            pltpu.VMEM((last_rows, pixels), F32),
-            pltpu.VMEM((last_rows, pixels), BF16),
-            pltpu.VMEM((last_rows, pixels), BF16),
+            pltpu.VMEM(spectra.shape, F32),
+            pltpu.VMEM(spectra.shape, BF16),
+            pltpu.VMEM(spectra.shape, BF16),
+            pltpu.VMEM((rank, pixels), F32),
+            pltpu.VMEM((rank, pixels), F32),
+            pltpu.VMEM((blocks, rank, LANES), F32),
+            pltpu.VMEM((2 * rank, pixels), BF16),
+            pltpu.VMEM((rank, positions), F32),
             pltpu.VMEM((rank, positions), F32),
             pltpu.VMEM((2 * rank, positions), BF16),
             pltpu.VMEM((positions // pos_chunk, rank, pos_chunk), F32),
@@ -444,17 +425,21 @@
             pltpu.VMEM((n, per, rows, LANES), F32),
             pltpu.VMEM((rank // pack, LANES), F32),
             pltpu.VMEM((n, rank // pack, LANES), F32),
-            dma((last_rows // chunk,)),
+            pltpu.SemaphoreType.REGULAR,
+            pltpu.SemaphoreType.REGULAR,
+            dma((positions // chunk,)),
+            dma((2,)),
+            dma((2,)),
             dma((2, positions // pos_chunk)),
             dma((2, half * LANES // col_chunk)),
             dma((n,)), dma((n,)), dma((n,)), dma((n,)),
             dma((n,)), dma((n,)), dma((n,)), dma((n,)),
         ],
         compiler_params=pltpu.CompilerParams(
-            collective_id=1, has_side_effects=True, vmem_limit_bytes=40 << 20
+            collective_id=0, has_side_effects=True, vmem_limit_bytes=40 << 20
         ),
         name="update",
-    )(inputs[0], *parts)
+    )(*inputs)
     return pl.pallas_call(
         functools.partial(output_kernel, n),
         out_shape=(

time: 25.4 us -> 25.1 us (0.988)
  Pallas kernels: 24.6 us -> 24.3 us
    pallas_call x2 -> x1, Pallas kernels: 23.8 us -> 23.5 us  [per_device(): pl.pallas_call(functools.partial(update_kernel, n, chunk, 3, pos_chunk, c...]
where the time goes in v2:
time: 25.1 us; the launch traced here: 24.9 us
  Pallas kernels  24.3 us (97%)
  between operations  0.64 us (3%)
    pallas_call x1, Pallas kernels, per_device(): pl.pallas_call(functools.partial(update_kernel, n, chunk, 3, pos_chunk, c...  23.5 us
    pallas_call x1, Pallas kernels, per_device(): pl.pallas_call(functools.partial(output_kernel, n), out_shape=(jax.ShapeD...  0.83 us

profile of v2, /device:TPU:0, one launch (start us, length us, event | category | flops | bytes accessed | tf_op | source)
XLA Modules:
  0.0 24.9 jit_solution(6492282524021619225)
XLA Ops:
  0.6 23.5 %update.1 = (f32[32,1024]{1,0:T(8,128)S(1)}, f32[8,1,32,128]{3,2,1,0:T(8,128)S(1)}, f32[8,1,32,128]{3,2,1,0:T(8,128)S(1)}) custom-call(f32[1024,2048]{1,0:T(8,128)} %spectra.1, f32[32,2048]{1,0:T(8,128)} %basis.1, f32[32,1024]{1,0:T(8,128)} %loadings.1), custom_call_target="tpu_custom_call" | custom-call | tf_op jit(solution)/shard_map/update/pallas_call | solution.py:400
  24.1 0.8 %write_out.1 = (f32[32,1024]{1,0:T(8,128)}, f32[32,2048]{1,0:T(8,128)}) custom-call(f32[32,1024]{1,0:T(8,128)S(1)} %get-tuple-element.5.fresh, f32[8,1,32,128]{3,2,1,0:T(8,128)S(1)} %get-tuple-element.6.ag_in, f32[8,1,32,128]{3,2,1,0:T(8,128)S(1)} %get-tuple-element.7.fw_in), custom_call_target="tpu_custom_call" | custom-call | tf_op jit(solution)/shard_map/write_out/pallas_call | solution.py:443

commit v3 on v2

--- a/solution.py
+++ b/solution.py
@@ -26,6 +26,12 @@
 
 def dot_nn(a, b):
     return lax.dot_general(a, b, (((1,), (0,)), ((), ())), preferred_element_type=F32)
+
+
+def product(a, b):
+    a_hi, a_lo = split(a)
+    b_hi, b_lo = split(b)
+    return dot_nn(a_hi, b_hi) + (dot_nn(a_hi, b_lo) + dot_nn(a_lo, b_hi))
 
 
 def mirrored(x):
@@ -65,7 +71,7 @@
 
 
 def update_kernel(
-    n, chunk, early, pos_chunk, col_chunk,
+    n, chunk, early, flight, pos_chunk, col_chunk,
     spectra, basis, loadings,
     new_loadings, ag_in, fw_in,
     sbuf, s_hi, s_lo, own, other, tied3, tied2, load, weighted,
@@ -131,13 +137,15 @@
             )
 
     own_copy.start()
-    for i in range(early, len(spectra_copies)):
+    load_copy.start()
+    for i in range(early, flight):
         spectra_copies[i].start()
-    load_copy.start()
 
     first_chunks = first_rows // chunk
     for i in range(first_chunks):
         spectra_copies[i].wait()
+        if i + flight < len(spectra_copies):
+            spectra_copies[i + flight].start()
         divide(sbuf, s_hi, s_lo, i * chunk, chunk)
     own_copy.wait()
     basis_copy.wait_recv()
@@ -166,15 +174,10 @@
             both[:, :rank] + (both[:, rank:] + low)
         ).T
 
+    for i in range(first_chunks + flight, len(spectra_copies)):
+        spectra_copies[i].start()
     for i in range(first_chunks):
         products(i * chunk)
-    squares = dot_nt(tied2[...], tied2[...])
-    gram = 2.0 * (
-        squares[:rank, :rank] + (squares[:rank, rank:] + squares[rank:, :rank])
-    )
-    weighted[...] = jnp.dot(
-        gram, load[...], precision=HIGHEST, preferred_element_type=F32
-    )
     for i in range(chunks // 2):
         num_copies[i].start()
     for copy in spectra_copies[first_chunks:]:
@@ -184,6 +187,12 @@
         if (i + 1) * chunk < positions:
             divide(sbuf, s_hi, s_lo, (i + 1) * chunk, chunk)
         products(i * chunk)
+        if i == first_chunks:
+            squares = dot_nt(tied2[...], tied2[...])
+            gram = 2.0 * (
+                squares[:rank, :rank] + (squares[:rank, rank:] + squares[rank:, :rank])
+            )
+            weighted[...] = product(gram, load[...])
     for i in range(chunks // 2, chunks):
         num_copies[i].start()
 
@@ -398,7 +407,7 @@
     hbm = pl.BlockSpec(memory_space=pltpu.HBM)
     inputs = [pltpu.with_memory_space_constraint(x, pltpu.HBM) for x in (spectra, basis, loadings)]
     outs = pl.pallas_call(
-        functools.partial(update_kernel, n, chunk, 3, pos_chunk, col_chunk),
+        functools.partial(update_kernel, n, chunk, 4, 4, pos_chunk, col_chunk),
         out_shape=(
             pltpu.VMEM(loadings.shape, F32),
             pltpu.VMEM((n, per, rows, LANES), F32),

time: 25.1 us -> 23.8 us (0.948)
  Pallas kernels: 24.3 us -> 23.1 us
    pallas_call x1, Pallas kernels: 23.5 us -> 22.2 us  [per_device(): pl.pallas_call(functools.partial(update_kernel, n, chunk, 4, 4, pos_chunk...]
where the time goes in v3:
time: 23.8 us; the launch traced here: 23.7 us
  Pallas kernels  23.1 us (97%)
  between operations  0.64 us (3%)
    pallas_call x1, Pallas kernels, per_device(): pl.pallas_call(functools.partial(update_kernel, n, chunk, 4, 4, pos_chunk...  22.2 us
    pallas_call x1, Pallas kernels, per_device(): pl.pallas_call(functools.partial(output_kernel, n), out_shape=(jax.ShapeD...  0.83 us

profile of v3, /device:TPU:0, one launch (start us, length us, event | category | flops | bytes accessed | tf_op | source)
XLA Modules:
  0.0 23.7 jit_solution(8061103727936384905)
XLA Ops:
  0.6 22.2 %update.1 = (f32[32,1024]{1,0:T(8,128)S(1)}, f32[8,1,32,128]{3,2,1,0:T(8,128)S(1)}, f32[8,1,32,128]{3,2,1,0:T(8,128)S(1)}) custom-call(f32[1024,2048]{1,0:T(8,128)} %spectra.1, f32[32,2048]{1,0:T(8,128)} %basis.1, f32[32,1024]{1,0:T(8,128)} %loadings.1), custom_call_target="tpu_custom_call" | custom-call | tf_op jit(solution)/shard_map/update/pallas_call | solution.py:409
  22.9 0.8 %write_out.1 = (f32[32,1024]{1,0:T(8,128)}, f32[32,2048]{1,0:T(8,128)}) custom-call(f32[32,1024]{1,0:T(8,128)S(1)} %get-tuple-element.5.fresh, f32[8,1,32,128]{3,2,1,0:T(8,128)S(1)} %get-tuple-element.6.ag_in, f32[8,1,32,128]{3,2,1,0:T(8,128)S(1)} %get-tuple-element.7.fw_in), custom_call_target="tpu_custom_call" | custom-call | tf_op jit(solution)/shard_map/write_out/pallas_call | solution.py:452

commit v4 on v3

--- a/solution.py
+++ b/solution.py
@@ -90,12 +90,21 @@
     partner = {"det": 1 - det}
     positions = load.shape[1]
     first_rows = positions // 2
+    first_chunks = first_rows // chunk
+    single = owners == n
 
     def peer(k):
         return lax.rem(me + k, n)
 
     def source(k):
         return lax.rem(me + n - k, n)
+
+    def slot(k):
+        return 0 if single else k
+
+    def group(buffer, send, recv):
+        part = pl.ds(1, n - 1)
+        return remote(buffer.at[part], buffer.at[part], send.at[0], recv.at[0], partner)
 
     def owner_only(index, fn):
         if owners == n:
@@ -113,8 +122,14 @@
     for i in range(positions // chunk):
         part = pl.ds(i * chunk, chunk)
         spectra_copies.append(
-            pltpu.make_async_copy(spectra.at[part], sbuf.at[part], sp_sem.at[i])
-        )
+            pltpu.make_async_copy(
+                spectra.at[part], sbuf.at[part], sp_sem.at[min(i, first_chunks)]
+            )
+        )
+    late_part = pl.ds(first_rows, positions - first_rows)
+    late_copy = pltpu.make_async_copy(
+        spectra.at[late_part], sbuf.at[late_part], sp_sem.at[first_chunks]
+    )
     own_copy = pltpu.make_async_copy(basis, own, io_sem.at[0])
     load_copy = pltpu.make_async_copy(loadings, load, io_sem.at[1])
     basis_copy = remote(basis, other, bs_sem.at[0], bs_sem.at[1], partner)
@@ -141,7 +156,6 @@
     for i in range(early, flight):
         spectra_copies[i].start()
 
-    first_chunks = first_rows // chunk
     for i in range(first_chunks):
         spectra_copies[i].wait()
         if i + flight < len(spectra_copies):
@@ -160,10 +174,12 @@
     load_copy.wait()
 
     chunks = positions // pos_chunk
-    num_copies = [
-        remote(num_out.at[i], num_in.at[i], nm_sem.at[0, i], nm_sem.at[1, i], partner)
-        for i in range(chunks)
-    ]
+    num_copies = []
+    for i in range(2):
+        part = pl.ds(i * (chunks // 2), chunks // 2)
+        num_copies.append(
+            remote(num_out.at[part], num_in.at[part], nm_sem.at[0, i], nm_sem.at[1, i], partner)
+        )
 
     def products(start):
         part = slice(start, start + chunk)
@@ -178,10 +194,8 @@
         spectra_copies[i].start()
     for i in range(first_chunks):
         products(i * chunk)
-    for i in range(chunks // 2):
-        num_copies[i].start()
-    for copy in spectra_copies[first_chunks:]:
-        copy.wait()
+    num_copies[0].start()
+    late_copy.wait()
     divide(sbuf, s_hi, s_lo, first_rows, chunk)
     for i in range(first_chunks, positions // chunk):
         if (i + 1) * chunk < positions:
@@ -193,11 +207,9 @@
                 squares[:rank, :rank] + (squares[:rank, rank:] + squares[rank:, :rank])
             )
             weighted[...] = product(gram, load[...])
-    for i in range(chunks // 2, chunks):
-        num_copies[i].start()
+    num_copies[1].start()
 
     def update(i):
-        num_copies[i].wait_recv()
         cols = slice(i * pos_chunk, (i + 1) * pos_chunk)
         fresh = load[:, cols] * (num_out[i] + num_in[i]) / weighted[:, cols]
         new_loadings[:, cols] = fresh
@@ -227,6 +239,7 @@
             remote(w_out.at[part], w_in.at[part], w_sem.at[0, i], w_sem.at[1, i], partner)
         )
     early_rows, late_rows = slice(0, first_rows), slice(first_rows, positions)
+    num_copies[0].wait_recv()
     for i in range(chunks // 2):
         update(i)
     for i in range(count):
@@ -239,6 +252,7 @@
         pl.semaphore_wait(barrier, n - 1)
         pl.semaphore_signal(ready, inc=1, device_id=partner, device_id_type=MESH)
 
+    num_copies[1].wait_recv()
     for i in range(chunks // 2, chunks):
         update(i)
     for i in range(count):
@@ -252,7 +266,7 @@
     cr_copies = [None]
     for k in range(1, n):
         cr_copies.append(
-            remote(cr_out, cr_in.at[k], cr_send.at[k], cr_recv.at[k], {"scan": peer(k)})
+            remote(cr_out, cr_in.at[k], cr_send.at[0], cr_recv.at[0], {"scan": peer(k)})
         )
     squares = dot_nt(nl2[...], nl2[...])
     cross = squares[:rank, :rank] + (squares[:rank, rank:] + squares[rank:, :rank])
@@ -270,7 +284,7 @@
         rs_copies.append(
             remote(
                 w_keep.at[piece_at(peer(k), per, row_split, rows)], rs_in.at[k],
-                rs_send.at[k], rs_recv.at[k], {"scan": peer(k)},
+                rs_send.at[slot(k)], rs_recv.at[slot(k)], {"scan": peer(k)},
             )
         )
     for i in range(count):
@@ -281,8 +295,7 @@
     for k in range(1, n):
         owner_only(peer(k), rs_copies[k].start)
 
-    for k in range(1, n):
-        cr_copies[k].wait_recv()
+    group(cr_in, cr_send, cr_recv).wait_recv()
     total = cr_out[...]
     for k in range(1, n):
         total = total + cr_in[k]
@@ -294,9 +307,9 @@
     ag_copies = [None]
     for k in range(1, n):
         ag_copies.append(
-            remote(piece_buf, ag_in.at[k], ag_send.at[k], ag_recv.at[k], {"scan": peer(k)})
-        )
-    if owners == n:
+            remote(piece_buf, ag_in.at[k], ag_send.at[slot(k)], ag_recv.at[slot(k)], {"scan": peer(k)})
+        )
+    if single:
         fw_copies = [remote(ag_in, fw_in, fw_send.at[0], fw_recv.at[0], partner)]
     else:
         fw_copies = [
@@ -318,8 +331,11 @@
                         piece_buf[0] = weights[i * rows:(i + 1) * rows]
             else:
                 piece_buf[j] = weights
-        for k in range(1, n):
-            rs_copies[k].wait_recv()
+        if single:
+            group(rs_in, rs_send, rs_recv).wait_recv()
+        else:
+            for k in range(1, n):
+                rs_copies[k].wait_recv()
         for j in range(per):
             total = w_keep[first.start + j, row, :]
             for k in range(1, n):
@@ -327,7 +343,7 @@
             piece_buf[j] = tied3[first.start + j, row, :] * (0.5 * total) / piece_buf[j]
         for k in range(1, n):
             ag_copies[k].start()
-        if owners < n:
+        if not single:
             fw_copies[0].start()
 
     owner_only(me, own_piece)
@@ -335,18 +351,21 @@
     def arrived(k):
         def go():
             ag_copies[k].wait_recv()
-            if owners < n:
-                fw_copies[k].start()
+            fw_copies[k].start()
         return go
 
-    for k in range(1, n):
-        owner_only(source(k), arrived(k))
-    if owners == n:
+    if single:
+        group(ag_in, ag_send, ag_recv).wait_recv()
         fw_copies[0].start()
-    for k in range(1, n):
-        cr_copies[k].wait_send()
-        owner_only(peer(k), rs_copies[k].wait_send)
-        owner_only(me, ag_copies[k].wait_send)
+        group(rs_in, rs_send, rs_recv).wait_send()
+        group(ag_in, ag_send, ag_recv).wait_send()
+    else:
+        for k in range(1, n):
+            owner_only(source(k), arrived(k))
+        for k in range(1, n):
+            owner_only(peer(k), rs_copies[k].wait_send)
+            owner_only(me, ag_copies[k].wait_send)
+    group(cr_in, cr_send, cr_recv).wait_send()
     for copy in [basis_copy] + num_copies + w_copies:
         copy.wait_send()
     for k, copy in enumerate(fw_copies):
@@ -397,6 +416,7 @@
     blocks = pixels // LANES
     half, per, row_split = layout(n, rank, pixels)
     rows = rank // row_split
+    slots = 1 if half // per * row_split == n else n
     chunk = positions // 8
     pos_chunk = positions // 4
     col_chunk = 4 * LANES
@@ -436,13 +456,13 @@
             pltpu.VMEM((n, rank // pack, LANES), F32),
             pltpu.SemaphoreType.REGULAR,
             pltpu.SemaphoreType.REGULAR,
-            dma((positions // chunk,)),
+            dma((positions // 2 // chunk + 1,)),
             dma((2,)),
             dma((2,)),
-            dma((2, positions // pos_chunk)),
+            dma((2, 2)),
             dma((2, half * LANES // col_chunk)),
-            dma((n,)), dma((n,)), dma((n,)), dma((n,)),
-            dma((n,)), dma((n,)), dma((n,)), dma((n,)),
+            dma((slots,)), dma((slots,)), dma((1,)), dma((1,)),
+            dma((slots,)), dma((slots,)), dma((slots,)), dma((slots,)),
         ],
         compiler_params=pltpu.CompilerParams(
             collective_id=0, has_side_effects=True, vmem_limit_bytes=40 << 20

time: 23.8 us -> 23.3 us (0.979)
  Pallas kernels: 23.1 us -> 22.5 us
    pallas_call x1, Pallas kernels: 22.2 us -> 21.7 us  [per_device(): pl.pallas_call(functools.partial(update_kernel, n, chunk, 4, 4, pos_chunk...]
where the time goes in v4:
time: 23.3 us; the launch traced here: 23.1 us
  Pallas kernels  22.5 us (97%)
  between operations  0.64 us (3%)
    pallas_call x1, Pallas kernels, per_device(): pl.pallas_call(functools.partial(update_kernel, n, chunk, 4, 4, pos_chunk...  21.7 us
    pallas_call x1, Pallas kernels, per_device(): pl.pallas_call(functools.partial(output_kernel, n), out_shape=(jax.ShapeD...  0.83 us

profile of v4, /device:TPU:0, one launch (start us, length us, event | category | flops | bytes accessed | tf_op | source)
XLA Modules:
  0.0 23.1 jit_solution(12820419346889009852)
XLA Ops:
  0.6 21.7 %update.1 = (f32[32,1024]{1,0:T(8,128)S(1)}, f32[8,1,32,128]{3,2,1,0:T(8,128)S(1)}, f32[8,1,32,128]{3,2,1,0:T(8,128)S(1)}) custom-call(f32[1024,2048]{1,0:T(8,128)} %spectra.1, f32[32,2048]{1,0:T(8,128)} %basis.1, f32[32,1024]{1,0:T(8,128)} %loadings.1), custom_call_target="tpu_custom_call" | custom-call | tf_op jit(solution)/shard_map/update/pallas_call | solution.py:429
  22.3 0.8 %write_out.1 = (f32[32,1024]{1,0:T(8,128)}, f32[32,2048]{1,0:T(8,128)}) custom-call(f32[32,1024]{1,0:T(8,128)S(1)} %get-tuple-element.5.fresh, f32[8,1,32,128]{3,2,1,0:T(8,128)S(1)} %get-tuple-element.6.ag_in, f32[8,1,32,128]{3,2,1,0:T(8,128)S(1)} %get-tuple-element.7.fw_in), custom_call_target="tpu_custom_call" | custom-call | tf_op jit(solution)/shard_map/write_out/pallas_call | solution.py:472

commit v5 on v4

--- a/solution.py
+++ b/solution.py
@@ -92,6 +92,7 @@
     first_rows = positions // 2
     first_chunks = first_rows // chunk
     single = owners == n
+    middle = max(n // 2, 1)
 
     def peer(k):
         return lax.rem(me + k, n)
@@ -307,10 +308,16 @@
     ag_copies = [None]
     for k in range(1, n):
         ag_copies.append(
-            remote(piece_buf, ag_in.at[k], ag_send.at[slot(k)], ag_recv.at[slot(k)], {"scan": peer(k)})
+            remote(piece_buf, ag_in.at[k], ag_send.at[slot(k)], ag_recv.at[k // middle if single else k], {"scan": peer(k)})
         )
     if single:
-        fw_copies = [remote(ag_in, fw_in, fw_send.at[0], fw_recv.at[0], partner)]
+        parts = [(low, min(low + middle, n)) for low in range(0, n, middle)]
+        fw_copies = []
+        for i, (low, high) in enumerate(parts):
+            part = pl.ds(low, high - low)
+            fw_copies.append(
+                remote(ag_in.at[part], fw_in.at[part], fw_send.at[i], fw_recv.at[i], partner)
+            )
     else:
         fw_copies = [
             remote(ag_in.at[k], fw_in.at[k], fw_send.at[k], fw_recv.at[k], partner)
@@ -355,8 +362,13 @@
         return go
 
     if single:
-        group(ag_in, ag_send, ag_recv).wait_recv()
-        fw_copies[0].start()
+        for i, (low, high) in reversed(list(enumerate(parts))):
+            part = pl.ds(max(low, 1), high - max(low, 1))
+            if high > max(low, 1):
+                remote(
+                    ag_in.at[part], ag_in.at[part], ag_send.at[0], ag_recv.at[i], partner
+                ).wait_recv()
+            fw_copies[i].start()
         group(rs_in, rs_send, rs_recv).wait_send()
         group(ag_in, ag_send, ag_recv).wait_send()
     else:
@@ -393,21 +405,26 @@
                 value = mirrored(value)
             nb[row, pl.ds(pl.multiple_of(block * LANES, LANES), LANES)] = value
 
-    for k in range(n):
-        index = lax.rem(me + n - k, n)
-
-        def go():
-            put(index, ag_in.at[k], False)
-            put(index, fw_in.at[k], True)
-
-        if owners == n:
-            go()
-        else:
-            pl.when(index < owners)(go)
-    second_copy = pltpu.make_async_copy(nb, new_basis, io_sem.at[1])
-    second_copy.start()
+    copies = []
+    for flip, ref in enumerate((ag_in, fw_in)):
+        for k in range(n):
+            index = lax.rem(me + n - k, n)
+
+            def go():
+                put(index, ref.at[k], flip)
+
+            if owners == n:
+                go()
+            else:
+                pl.when(index < owners)(go)
+        part = pl.ds(flip * (pixels // 2), pixels // 2)
+        copies.append(
+            pltpu.make_async_copy(nb.at[:, part], new_basis.at[:, part], io_sem.at[1 + flip])
+        )
+        copies[flip].start()
     first_copy.wait()
-    second_copy.wait()
+    for copy in copies:
+        copy.wait()
 
 
 def per_device(n, spectra, basis, loadings):
@@ -462,7 +479,7 @@
             dma((2, 2)),
             dma((2, half * LANES // col_chunk)),
             dma((slots,)), dma((slots,)), dma((1,)), dma((1,)),
-            dma((slots,)), dma((slots,)), dma((slots,)), dma((slots,)),
+            dma((slots,)), dma((max(slots, 2),)), dma((max(slots, 2),)), dma((max(slots, 2),)),
         ],
         compiler_params=pltpu.CompilerParams(
             collective_id=0, has_side_effects=True, vmem_limit_bytes=40 << 20
@@ -477,7 +494,7 @@
         ),
         in_specs=[vmem] * 3,
         out_specs=(any_space,) * 2,
-        scratch_shapes=[pltpu.VMEM((rank, pixels), F32), dma((2,))],
+        scratch_shapes=[pltpu.VMEM((rank, pixels), F32), dma((3,))],
         compiler_params=pltpu.CompilerParams(vmem_limit_bytes=8 << 20),
         name="write_out",
     )(*outs)

time: 23.3 us -> 23.2 us (level)
  no operation moved by 1% of the time
where the time goes in v5:
time: 23.2 us; the launch traced here: 23 us
  Pallas kernels  22.4 us (97%)
  between operations  0.64 us (3%)
    pallas_call x1, Pallas kernels, per_device(): pl.pallas_call(functools.partial(update_kernel, n, chunk, 4, 4, pos_chunk...  21.6 us
    pallas_call x1, Pallas kernels, per_device(): pl.pallas_call(functools.partial(output_kernel, n), out_shape=(jax.ShapeD...  0.79 us

profile of v5, /device:TPU:0, one launch (start us, length us, event | category | flops | bytes accessed | tf_op | source)
XLA Modules:
  0.0 23.0 jit_solution(2703878524624524626)
XLA Ops:
  0.6 21.6 %update.1 = (f32[32,1024]{1,0:T(8,128)S(1)}, f32[8,1,32,128]{3,2,1,0:T(8,128)S(1)}, f32[8,1,32,128]{3,2,1,0:T(8,128)S(1)}) custom-call(f32[1024,2048]{1,0:T(8,128)} %spectra.1, f32[32,2048]{1,0:T(8,128)} %basis.1, f32[32,1024]{1,0:T(8,128)} %loadings.1), custom_call_target="tpu_custom_call" | custom-call | tf_op jit(solution)/shard_map/update/pallas_call | solution.py:446
  22.2 0.8 %write_out.1 = (f32[32,1024]{1,0:T(8,128)}, f32[32,2048]{1,0:T(8,128)}) custom-call(f32[32,1024]{1,0:T(8,128)S(1)} %get-tuple-element.5.fresh, f32[8,1,32,128]{3,2,1,0:T(8,128)S(1)} %get-tuple-element.6.ag_in, f32[8,1,32,128]{3,2,1,0:T(8,128)S(1)} %get-tuple-element.7.fw_in), custom_call_target="tpu_custom_call" | custom-call | tf_op jit(solution)/shard_map/write_out/pallas_call | solution.py:489

commit v6 on v5

--- a/solution.py
+++ b/solution.py
@@ -182,19 +182,19 @@
             remote(num_out.at[part], num_in.at[part], nm_sem.at[0, i], nm_sem.at[1, i], partner)
         )
 
-    def products(start):
-        part = slice(start, start + chunk)
+    def products(start, size=chunk):
+        part = slice(start, start + size)
         both = dot_nt(s_hi[part, :], tied2[...])
         low = dot_nt(s_lo[part, :], tied2[:rank, :])
         at = start % pos_chunk
-        num_out[start // pos_chunk, :, at:at + chunk] = (
+        num_out[start // pos_chunk, :, at:at + size] = (
             both[:, :rank] + (both[:, rank:] + low)
         ).T
 
     for i in range(first_chunks + flight, len(spectra_copies)):
         spectra_copies[i].start()
-    for i in range(first_chunks):
-        products(i * chunk)
+    for start in range(0, first_rows, pos_chunk):
+        products(start, pos_chunk)
     num_copies[0].start()
     late_copy.wait()
     divide(sbuf, s_hi, s_lo, first_rows, chunk)

time: 23.2 us -> 23.2 us (level)
  no operation moved by 1% of the time
where the time goes in v6:
time: 23.2 us; the launch traced here: 23 us
  Pallas kernels  22.4 us (97%)
  between operations  0.64 us (3%)
    pallas_call x1, Pallas kernels, per_device(): pl.pallas_call(functools.partial(update_kernel, n, chunk, 4, 4, pos_chunk...  21.6 us
    pallas_call x1, Pallas kernels, per_device(): pl.pallas_call(functools.partial(output_kernel, n), out_shape=(jax.ShapeD...  0.79 us

profile of v6, /device:TPU:0, one launch (start us, length us, event | category | flops | bytes accessed | tf_op | source)
XLA Modules:
  0.0 23.0 jit_solution(13033362541274332618)
XLA Ops:
  0.6 21.6 %update.1 = (f32[32,1024]{1,0:T(8,128)S(1)}, f32[8,1,32,128]{3,2,1,0:T(8,128)S(1)}, f32[8,1,32,128]{3,2,1,0:T(8,128)S(1)}) custom-call(f32[1024,2048]{1,0:T(8,128)} %spectra.1, f32[32,2048]{1,0:T(8,128)} %basis.1, f32[32,1024]{1,0:T(8,128)} %loadings.1), custom_call_target="tpu_custom_call" | custom-call | tf_op jit(solution)/shard_map/update/pallas_call | solution.py:446
  22.2 0.8 %write_out.1 = (f32[32,1024]{1,0:T(8,128)}, f32[32,2048]{1,0:T(8,128)}) custom-call(f32[32,1024]{1,0:T(8,128)S(1)} %get-tuple-element.5.fresh, f32[8,1,32,128]{3,2,1,0:T(8,128)S(1)} %get-tuple-element.6.ag_in, f32[8,1,32,128]{3,2,1,0:T(8,128)S(1)} %get-tuple-element.7.fw_in), custom_call_target="tpu_custom_call" | custom-call | tf_op jit(solution)/shard_map/write_out/pallas_call | solution.py:489

commit v7 on v5

--- a/solution.py
+++ b/solution.py
@@ -293,8 +293,13 @@
         for j in range(step):
             b = half - 1 - (i * step + j)
             w_keep[b] = w_keep[b] + mirrored(w_in[half - 1 - b])
-    for k in range(1, n):
-        owner_only(peer(k), rs_copies[k].start)
+        if step % per:
+            low, high = (0, half) if i == count - 1 else (0, 0)
+        else:
+            low, high = half - (i + 1) * step, half - i * step
+        for k in range(1, n):
+            first = peer(k) // row_split * per
+            pl.when((first >= low) & (first < high))(rs_copies[k].start)
 
     group(cr_in, cr_send, cr_recv).wait_recv()
     total = cr_out[...]

time: 23.2 us -> 23.3 us (level)
  no operation moved by 1% of the time
where the time goes in v7:
time: 23.3 us; the launch traced here: 23.2 us
  Pallas kernels  22.6 us (97%)
  between operations  0.64 us (3%)
    pallas_call x1, Pallas kernels, per_device(): pl.pallas_call(functools.partial(update_kernel, n, chunk, 4, 4, pos_chunk...  21.8 us
    pallas_call x1, Pallas kernels, per_device(): pl.pallas_call(functools.partial(output_kernel, n), out_shape=(jax.ShapeD...  0.79 us

profile of v7, /device:TPU:0, one launch (start us, length us, event | category | flops | bytes accessed | tf_op | source)
XLA Modules:
  0.0 23.2 jit_solution(13183079492711222396)
XLA Ops:
  0.6 21.8 %update.1 = (f32[32,1024]{1,0:T(8,128)S(1)}, f32[8,1,32,128]{3,2,1,0:T(8,128)S(1)}, f32[8,1,32,128]{3,2,1,0:T(8,128)S(1)}) custom-call(f32[1024,2048]{1,0:T(8,128)} %spectra.1, f32[32,2048]{1,0:T(8,128)} %basis.1, f32[32,1024]{1,0:T(8,128)} %loadings.1), custom_call_target="tpu_custom_call" | custom-call | tf_op jit(solution)/shard_map/update/pallas_call | solution.py:451
  22.4 0.8 %write_out.1 = (f32[32,1024]{1,0:T(8,128)}, f32[32,2048]{1,0:T(8,128)}) custom-call(f32[32,1024]{1,0:T(8,128)S(1)} %get-tuple-element.5.fresh, f32[8,1,32,128]{3,2,1,0:T(8,128)S(1)} %get-tuple-element.6.ag_in, f32[8,1,32,128]{3,2,1,0:T(8,128)S(1)} %get-tuple-element.7.fw_in), custom_call_target="tpu_custom_call" | custom-call | tf_op jit(solution)/shard_map/write_out/pallas_call | solution.py:494
